TPU v7x, 512 devices: a whole 4x4x16 slice. The times are simulated.
512 devices in a mesh: frames: 64 (over z, y), strips: 8 (over x, core).
Axes of the slice: x: 4, y: 4, z: 16, core: 2. Of those that a mesh axis runs over, the one named last changes fastest.
Arguments:
- raw_frames: bfloat16 [4096, 512, 512], P('frames', 'strips'), may hold values from -24 to 24
- dark_frame: float32 [512, 512], P('strips'), may hold values from -6 to 6
- dead_mask: int32 [512, 512], P('strips'), may hold values 0 or 1
- frame_group: int32 [4096], P('frames'), may hold values from 0 to 7
- prior_sigma: float32 [128], replicated, may hold values from 0.2 to 0.5
- start_rotation: float32 [128, 128], replicated, as said below
- basis: bfloat16 [262144, 128], P(('strips', 'frames')), may hold values from -0.01171875 to 0.01171875
Outputs:
- new_basis: bfloat16 [262144, 128], P(('strips', 'frames'))
- new_coeffs: float32 [4096, 128], P('frames')
- new_sigma: float32 [128], replicated
Inputs may be any that keep to these rules, and one draw needn't show every extreme that they name: start_rotation is nonsingular.
All inputs are finite; a program needn't handle non-finite values. No bound on the sum of `dead_mask` on one device may be relied on, other than what follows from the above.
Results may differ from a plain program's by a relative error of at most 0.0071.
Values may be sent and summed in bfloat16 or wider, within the bound.
A program may use at most 64 MiB of HBM per device.

v0:
```python
import jax
import jax.numpy as jnp
from jax import lax
from jax.sharding import PartitionSpec as P

GROUPS = 8
ITERS = 4
BLUR_TAPS = (1.0 / 64, 6.0 / 64, 15.0 / 64, 20.0 / 64, 15.0 / 64, 6.0 / 64, 1.0 / 64)
DECAY_RATE = 0.7


def extended(shard, sides, width):
    for axis, dim in sides:
        size, length = (lax.axis_size(axis), shard.shape[dim])
        up = [(i, (i + 1) % size) for i in range(size - 1)]
        down = [(j, i) for i, j in up]
        last = lax.slice_in_dim(shard, length - width, length, axis=dim)
        first = lax.slice_in_dim(shard, 0, width, axis=dim)
        before = lax.ppermute(last, axis, up)
        after = lax.ppermute(first, axis, down)
        shard = jnp.concatenate([before, shard, after], axis=dim)
    return shard


def orthonormalize(product):
    normal = jnp.dot(product.T, product, precision=lax.Precision.HIGHEST)
    factor = jnp.linalg.cholesky(normal)
    return lax.linalg.triangular_solve(
        factor, product, left_side=False, lower=True, transpose_a=True
    )


def body(raw_frames, dark_frame, dead_mask, frame_group, prior_sigma, start_rotation, basis):
    frame_count, strip_rows, columns = raw_frames.shape
    corrected = (
        (raw_frames.astype(jnp.float32) - dark_frame) * (1 - dead_mask).astype(jnp.float32)
    ).astype(jnp.bfloat16)
    position = jnp.arange(columns)
    offsets = position[None, :] - position[:, None]
    banded = jnp.zeros((columns, columns), jnp.float32)
    for shift_by in range(-3, 4):
        banded = banded + jnp.where(offsets == shift_by, BLUR_TAPS[shift_by + 3], 0.0)
    banded = banded.astype(jnp.bfloat16)
    column_blur = jnp.dot(
        corrected.reshape(frame_count * strip_rows, columns),
        banded,
        preferred_element_type=jnp.float32,
    )
    column_blur = column_blur.reshape(frame_count, strip_rows, columns)
    padded = extended(column_blur, (("strips", 1),), 3)
    row_blur = BLUR_TAPS[0] * padded[:, 0:strip_rows, :]
    for offset in range(1, 7):
        row_blur = row_blur + BLUR_TAPS[offset] * padded[:, offset : offset + strip_rows, :]
    frame_weight = jnp.power(
        jnp.float32(DECAY_RATE), (GROUPS - 1 - frame_group).astype(jnp.float32)
    )
    weighted = (
        (frame_weight[:, None, None] * row_blur)
        .astype(jnp.bfloat16)
        .reshape(frame_count, strip_rows * columns)
    )
    partial_value = jnp.dot(
        weighted,
        lax.all_gather(basis, "frames", axis=0, tiled=True),
        preferred_element_type=jnp.float32,
    )
    coeffs = lax.psum(partial_value, "strips")
    total_frames = frame_count * lax.axis_size("frames")
    local_gram = jnp.dot(coeffs.T, coeffs, precision=lax.Precision.HIGHEST)
    summed_gram = lax.psum(local_gram, "frames")
    gram = jnp.diag(prior_sigma * prior_sigma) + summed_gram / total_frames
    rotation = start_rotation
    for step in range(ITERS):
        rotation = orthonormalize(jnp.dot(gram, rotation, precision=lax.Precision.HIGHEST))
    new_coeffs = jnp.dot(coeffs, rotation, precision=lax.Precision.HIGHEST)
    new_basis = jnp.dot(
        basis.astype(jnp.float32), rotation, precision=lax.Precision.HIGHEST
    ).astype(jnp.bfloat16)
    curved = jnp.dot(gram, rotation, precision=lax.Precision.HIGHEST)
    new_sigma = jnp.sqrt(jnp.sum(rotation * curved, axis=0))
    return (new_basis, new_coeffs, new_sigma)


def solution(mesh):
    placed = (
        P("frames", "strips", None),
        P("strips", None),
        P("strips", None),
        P("frames"),
        P(),
        P(),
        P(("strips", "frames"), None),
    )
    return jax.shard_map(
        body,
        mesh=mesh,
        in_specs=placed,
        out_specs=(P(("strips", "frames"), None), P("frames", None), P()),
        check_vma=False,
    )
```

profile of v0, /device:TPU:2, one launch (start us, length us, event | category | flops | bytes accessed | tf_op | source)
XLA Modules:
  0.0 562.9 jit_solution(2204300600447689643)
XLA Ops:
  7.2 0.0 copy-start
  7.2 0.0 all-gather.2.cloned.1.call-start
  7.2 0.7 all-gather.2.cloned.1.call-update
  7.9 0.0 all-reduce.2.cloned.1.call-start
  8.0 0.9 subtract_convert_fusion
  8.9 0.0 copy-start.2
  8.9 4.7 fusion.18
  13.6 0.2 fusion.85
  13.9 1.9 collective-permute-start
  15.8 3.6 collective-permute-start.1
  19.5 0.0 copy-done.2
  19.5 4.9 collective-permute-done
  24.4 1.8 collective-permute-done.1
  26.1 8.9 %fusion.5 = bf16[64,64,512]{2,1,0:T(8,128)(2,1)S(1)} fusion(f32[64,64,512]{2,1,0:T(8,128)S(1)} %fusion.18, f32[64,3,512]{2,1,0:T(4,128)S(1)} %collective-permute-done.1, f32[64,3,512]{2,1,0:T(4,128)S(1)} %collective-permute-done, f32[64]{0:T(128)S(1)} %convert_power_fusion), kind=kLoop, calls=%fused_computation.13 | loop fusion | flops 44040192 | bytes 13369600 | tf_op jit(solution)/shard_map/convert_element_type | solution.py:59
  35.0 4.5 copy.15
  39.6 132.9 %all-gather.2.cloned.1.call-done = bf16[32768,128]{1,0:T(8,128)(2,1)} async-done(((bf16[512,128]{1,0:T(8,128)(2,1)}), bf16[32768,128]{1,0:T(8,128)(2,1)}) %all-gather.2.cloned.1.call-update) | async-done | bytes 8388624 | tf_op jit(solution)/shard_map/all_gather | solution.py:64
  172.4 0.0 copy-start.3
  172.4 0.0 copy-start.1
  172.4 6.3 %fusion.86 = f32[64,128]{1,0:T(8,128)S(1)} fusion(bf16[64,32768]{1,0:T(8,128)(2,1)} %bitcast.76, bf16[32768,128]{1,0:T(8,128)(2,1)} %all-gather.2.cloned.1.call-done), kind=kOutput, calls=%fused_computation.116 | convolution fusion | flops 536870912 | bytes 12615680 | tf_op jit(solution)/shard_map/dot_general | solution.py:62
  178.7 20.7 %psum.14 = f32[64,128]{1,0:T(8,128)S(1)} all-reduce(f32[64,128]{1,0:T(8,128)S(1)} %fusion.86), channel_id=1, replica_groups=mesh['frames'=64,'strips'=8] {'strips'}, use_global_device_ids=true, to_apply=%region_0.1 | all-reduce | flops 8192 | bytes 65536 | tf_op jit(solution)/shard_map/psum | solution.py:67
  199.4 0.9 fusion.87
  200.3 0.0 all-reduce.2.cloned.1.call-update
  200.3 0.0 copy-done.3
  200.4 253.0 %all-reduce.2.cloned.1.call-done = f32[128,128]{1,0:T(8,128)} async-done(((f32[128,128]{1,0:T(8,128)}), f32[128,128]{1,0:T(8,128)}) %all-reduce.2.cloned.1.call-update) | async-done | bytes 65552 | tf_op jit(solution)/shard_map/psum | solution.py:70
  453.4 0.0 copy-done
  453.4 1.1 fusion.83
  454.5 0.3 fusion.88
  454.8 0.1 copy.10
  454.9 11.7 %cholesky.74 = f32[128,128]{1,0:T(8,128)S(1)} custom-call(f32[128,128]{1,0:T(8,128)S(1)} %fusion.55), custom_call_target="Cholesky" | custom-call | tf_op jit(solution)/shard_map/jit(cholesky)/cholesky | solution.py:27
  466.6 0.6 compare_reduce_fusion.3
  467.3 0.7 fusion.44
  468.0 9.8 %custom-call.8 = f32[1,128,128]{1,2,0:T(8,128)S(1)} custom-call(f32[1,128,128]{2,1,0:T(8,128)S(1)} %fusion.44), custom_call_target="InvertDiagBlocksLowerTriangular" | custom-call | tf_op jit(solution)/shard_map/triangular_solve/custom-call.0 | solution.py:28
  477.8 0.3 convolution_bitcast_fusion.3
  478.1 1.1 fusion.81
  479.2 0.3 fusion.89
  479.5 0.1 copy.11
  479.6 11.7 %cholesky.85 = f32[128,128]{1,0:T(8,128)S(1)} custom-call(f32[128,128]{1,0:T(8,128)S(1)} %fusion.53), custom_call_target="Cholesky" | custom-call | tf_op jit(solution)/shard_map/jit(cholesky)/cholesky | solution.py:27
  491.4 0.6 compare_reduce_fusion.2
  492.0 0.7 fusion.45
  492.7 10.0 %custom-call.9 = f32[1,128,128]{1,2,0:T(8,128)S(1)} custom-call(f32[1,128,128]{2,1,0:T(8,128)S(1)} %fusion.45), custom_call_target="InvertDiagBlocksLowerTriangular" | custom-call | tf_op jit(solution)/shard_map/triangular_solve/custom-call.0 | solution.py:28
  502.7 0.3 convolution_bitcast_fusion.2
  503.0 1.1 fusion.79
  504.1 0.3 fusion.90
  504.4 0.1 copy.12
  504.5 11.7 %cholesky.96 = f32[128,128]{1,0:T(8,128)S(1)} custom-call(f32[128,128]{1,0:T(8,128)S(1)} %fusion.51), custom_call_target="Cholesky" | custom-call | tf_op jit(solution)/shard_map/jit(cholesky)/cholesky | solution.py:27
  516.3 0.6 compare_reduce_fusion.1
  516.9 0.7 fusion.46
  517.6 9.8 %custom-call.10 = f32[1,128,128]{1,2,0:T(8,128)S(1)} custom-call(f32[1,128,128]{2,1,0:T(8,128)S(1)} %fusion.46), custom_call_target="InvertDiagBlocksLowerTriangular" | custom-call | tf_op jit(solution)/shard_map/triangular_solve/custom-call.0 | solution.py:28
  527.4 0.3 convolution_bitcast_fusion.1
  527.7 1.1 fusion.77
  528.8 0.3 fusion.91
  529.1 0.1 copy.13
  529.2 11.7 %cholesky.107 = f32[128,128]{1,0:T(8,128)S(1)} custom-call(f32[128,128]{1,0:T(8,128)S(1)} %fusion.49), custom_call_target="Cholesky" | custom-call | tf_op jit(solution)/shard_map/jit(cholesky)/cholesky | solution.py:27
  541.0 0.6 compare_reduce_fusion
  541.6 0.7 fusion.47
  542.3 10.0 %custom-call.11 = f32[1,128,128]{1,2,0:T(8,128)S(1)} custom-call(f32[1,128,128]{2,1,0:T(8,128)S(1)} %fusion.47), custom_call_target="InvertDiagBlocksLowerTriangular" | custom-call | tf_op jit(solution)/shard_map/triangular_solve/custom-call.0 | solution.py:28
  552.3 0.2 convolution_bitcast_fusion
  552.5 0.8 fusion.92
  553.3 0.0 copy-done.1
  553.3 0.3 fusion.21
  553.6 1.1 fusion.22
  554.7 0.5 sqrt.3
  555.3 0.8 copy.14
  (10 shorter events, 0.2 us)
Async XLA Ops:
  7.2 446.2 %copy-start = (f32[128,128]{1,0:T(8,128)S(1)}, f32[128,128]{1,0:T(8,128)}, u32[]{:S(2)}) copy-start(f32[128,128]{1,0:T(8,128)} %param.15) | copy-start | bytes 196612
  7.2 165.3 %all-gather.2.cloned.1.call-start = ((), (), s32[]{:S(2)}) async-start(), calls=%async_computation | async-start | bytes 8519680 | tf_op jit(solution)/shard_map/all_gather | solution.py:64
  7.9 445.5 %all-reduce.2.cloned.1.call-start = ((), (), s32[]{:S(2)}) async-start(), calls=%async_computation.1 | async-start | bytes 131072 | tf_op jit(solution)/shard_map/psum | solution.py:70
  8.9 10.6 %copy-start.2 = (s32[64]{0:T(128)S(1)}, s32[64]{0:T(128)}, u32[]{:S(2)}) copy-start(s32[64]{0:T(128)} %param.13) | copy-start | bytes 772
  13.9 10.5 %collective-permute-start = (f32[64,3,512]{2,1,0:T(4,128)S(1)}, f32[64,3,512]{2,1,0:T(4,128)S(1)}, u32[]{:S(2)}, u32[]{:S(2)}) collective-permute-start(f32[64,3,512]{2,1,0:T(4,128)S(1)} %get-tuple-element.8), channel_id=1, source_target_pairs={{0,1},{1,2},{2,3},{3,4},{4,5},{5,6},{6,7},{8,9},{9,10},{10,11},{11... | collective-permute-start | bytes 1179656 | tf_op jit(solution)/shard_map/ppermute | solution.py:19
  15.8 10.3 %collective-permute-start.1 = (f32[64,3,512]{2,1,0:T(4,128)S(1)}, f32[64,3,512]{2,1,0:T(4,128)S(1)}, u32[]{:S(2)}, u32[]{:S(2)}) collective-permute-start(f32[64,3,512]{2,1,0:T(4,128)S(1)} %get-tuple-element.9), channel_id=1, source_target_pairs={{1,0},{2,1},{3,2},{4,3},{5,4},{6,5},{7,6},{9,8},{10,9},{11,10},{12... | collective-permute-start | bytes 1179656 | tf_op jit(solution)/shard_map/ppermute | solution.py:20
  172.4 27.9 %copy-start.3 = (f32[128]{0:T(128)S(1)}, f32[128]{0:T(128)}, u32[]{:S(2)}) copy-start(f32[128]{0:T(128)} %param.14) | copy-start | bytes 1540
  172.4 380.9 %copy-start.1 = (bf16[512,128]{1,0:T(8,128)(2,1)S(1)}, bf16[512,128]{1,0:T(8,128)(2,1)}, u32[]{:S(2)}) copy-start(bf16[512,128]{1,0:T(8,128)(2,1)} %param.16) | copy-start | bytes 393220
Sparse Core Ops, SparseCore 0:
  11.0 161.4 all-gather.1
  200.5 252.8 all-reduce.1
where the time goes:
time: 563 us
  waiting for transfers between devices  393 us (70%)
  other arithmetic  102 us (18%)
  matrix products  20.9 us (4%)
  blocking collectives  20.7 us (4%)
  between operations  14.3 us (3%)
  local copies, waits for them, and re-layouts  6.45 us (1%)
  starting transfers between devices  5.64 us (1%)
    psum x1, waiting for transfers between devices, body(): summed_gram = lax.psum(local_gram, 'frames')  253 us
    all_gather x1, waiting for transfers between devices, body(): lax.all_gather(basis, 'frames', axis=0, tiled=True)  133 us
    another operation x12, other arithmetic, orthonormalize(): factor = jnp.linalg.cholesky(normal)  49.6 us
    another operation x8, other arithmetic, orthonormalize(): lax.linalg.triangular_solve(factor, product, left_side=False, lower=True,...  42.2 us
    psum x1, blocking collectives, body(): coeffs = lax.psum(partial_value, 'strips')  20.7 us
  transfers between devices with their start and end apart: 4, of which 4 were waited for; matrix products, arithmetic and copies ran while one was open for 3% of the time, Pallas kernels for 0%

commit v1 on v0

--- a/solution.py
+++ b/solution.py
@@ -61,7 +61,9 @@
     )
     partial_value = jnp.dot(
         weighted,
-        lax.all_gather(basis, "frames", axis=0, tiled=True),
+        jnp.concatenate(
+            lax.all_to_all(jnp.stack([basis] * lax.axis_size("frames")), "frames", 0, 0), axis=0
+        ),
         preferred_element_type=jnp.float32,
     )
     coeffs = lax.psum(partial_value, "strips")

time: 563 us -> 804 us (1.43); the launches traced: 563 us -> 795 us
  waiting for transfers between devices: 393 us -> 601 us
  starting transfers between devices: 5.64 us -> 24.7 us
    all_to_all x0 -> x1, waiting for transfers between devices: none -> 343 us  [body(): lax.all_to_all(jnp.stack([basis] * lax.axis_size('frames')), 'frames', 0, 0)]
    all_gather x1 -> x0, waiting for transfers between devices: 133 us -> none  [body(): lax.all_gather(basis, 'frames', axis=0, tiled=True)]
    all_to_all x0 -> x1, starting transfers between devices: none -> 19.1 us  [body(): lax.all_to_all(jnp.stack([basis] * lax.axis_size('frames')), 'frames', 0, 0)]
  transfers between devices with their start and end apart: 4 -> 4, of which waited for: 4 -> 4; matrix products, arithmetic and copies ran while one was open for 3% -> 2% of each run, Pallas kernels for 0% -> 0%
where the time goes in v1:
time: 804 us; the launch traced here: 795 us
  waiting for transfers between devices  601 us (75%)
  other arithmetic  102 us (13%)
  starting transfers between devices  24.7 us (3%)
  matrix products  24.4 us (3%)
  blocking collectives  20.8 us (3%)
  between operations  14.8 us (2%)
  local copies, waits for them, and re-layouts  8.09 us (1%)
    all_to_all x1, waiting for transfers between devices, body(): lax.all_to_all(jnp.stack([basis] * lax.axis_size('frames')), 'frames', 0, 0)  343 us
    psum x1, waiting for transfers between devices, body(): summed_gram = lax.psum(local_gram, 'frames')  251 us
    another operation x12, other arithmetic, orthonormalize(): factor = jnp.linalg.cholesky(normal)  49.6 us
    another operation x8, other arithmetic, orthonormalize(): lax.linalg.triangular_solve(factor, product, left_side=False, lower=True,...  42.3 us
    psum x1, blocking collectives, body(): coeffs = lax.psum(partial_value, 'strips')  20.8 us
    all_to_all x1, starting transfers between devices, body(): lax.all_to_all(jnp.stack([basis] * lax.axis_size('frames')), 'frames', 0, 0)  19.1 us
  transfers between devices with their start and end apart: 4, of which 4 were waited for; matrix products, arithmetic and copies ran while one was open for 2% of the time, Pallas kernels for 0%

profile of v1, /device:TPU:2, one launch (start us, length us, event | category | flops | bytes accessed | tf_op | source)
XLA Modules:
  0.0 795.2 jit_solution(4203248741519737138)
XLA Ops:
  7.2 0.0 copy-start
  7.2 6.2 stack.2
  13.3 0.0 copy-start.2
  13.4 0.0 copy-start.3
  13.4 19.1 %all-to-all-start = ((bf16[64,512,128]{2,1,0:T(8,128)(2,1)}), bf16[64,512,128]{2,1,0:T(8,128)(2,1)}, u32[]{:S(2)}, u32[]{:S(2)}) async-start(bf16[64,512,128]{2,1,0:T(8,128)(2,1)} %stack.2), calls=%async_computation | async-start | bytes 16777216 | tf_op jit(solution)/shard_map/all_to_all | solution.py:65
  32.5 0.0 all-reduce.2.cloned.1.call-start
  32.5 0.0 copy-done.2
  32.6 0.0 copy-done.3
  32.6 0.0 copy-start.4
  32.6 4.8 fusion.18
  37.4 0.2 fusion.90
  37.6 1.9 collective-permute-start
  39.5 3.6 collective-permute-start.1
  43.2 0.0 copy-done.4
  43.2 4.9 collective-permute-done
  48.1 1.8 collective-permute-done.1
  49.9 9.7 %fusion.5 = bf16[64,64,512]{2,1,0:T(8,128)(2,1)} fusion(f32[64,64,512]{2,1,0:T(8,128)S(1)} %fusion.18, f32[64,3,512]{2,1,0:T(4,128)S(1)} %collective-permute-done.1, f32[64,3,512]{2,1,0:T(4,128)S(1)} %collective-permute-done, f32[64]{0:T(128)S(1)} %convert_power_fusion), kind=kLoop, calls=%fused_computation.13 | loop fusion | flops 44040192 | bytes 13369600 | tf_op jit(solution)/shard_map/convert_element_type | solution.py:59
  59.6 0.0 copy-start.5
  59.6 342.7 %all-to-all-done = bf16[64,512,128]{2,1,0:T(8,128)(2,1)} async-done(((bf16[64,512,128]{2,1,0:T(8,128)(2,1)}), bf16[64,512,128]{2,1,0:T(8,128)(2,1)}, u32[]{:S(2)}, u32[]{:S(2)}) %all-to-all-start) | async-done | bytes 8388640 | tf_op jit(solution)/shard_map/all_to_all | solution.py:65
  402.3 9.8 %fusion.25 = f32[64,128]{1,0:T(8,128)S(1)} fusion(bf16[64,512,128]{2,1,0:T(8,128)(2,1)} %all-to-all-done, bf16[64,64,512]{2,1,0:T(8,128)(2,1)} %fusion.5), kind=kOutput, calls=%fused_computation.42 | convolution fusion | flops 536870912 | bytes 12615680 | tf_op jit(solution)/shard_map/dot_general | solution.py:62
  412.0 20.8 %psum.14 = f32[64,128]{1,0:T(8,128)S(1)} all-reduce(f32[64,128]{1,0:T(8,128)S(1)} %fusion.25), channel_id=1, replica_groups=mesh['frames'=64,'strips'=8] {'strips'}, use_global_device_ids=true, to_apply=%region_0.1 | all-reduce | flops 8192 | bytes 65536 | tf_op jit(solution)/shard_map/psum | solution.py:69
  432.8 0.9 fusion.91
  433.8 0.0 all-reduce.2.cloned.1.call-update
  433.8 0.0 copy-done.5
  433.8 251.5 %all-reduce.2.cloned.1.call-done = f32[128,128]{1,0:T(8,128)} async-done(((f32[128,128]{1,0:T(8,128)}), f32[128,128]{1,0:T(8,128)}) %all-reduce.2.cloned.1.call-update) | async-done | bytes 65552 | tf_op jit(solution)/shard_map/psum | solution.py:72
  685.3 0.0 copy-done
  685.3 1.1 fusion.88
  686.4 0.3 fusion.92
  686.7 0.1 copy.11
  686.8 11.7 %cholesky.74 = f32[128,128]{1,0:T(8,128)S(1)} custom-call(f32[128,128]{1,0:T(8,128)S(1)} %fusion.60), custom_call_target="Cholesky" | custom-call | tf_op jit(solution)/shard_map/jit(cholesky)/cholesky | solution.py:27
  698.5 0.6 compare_reduce_fusion.3
  699.2 0.7 fusion.49
  699.8 9.8 %custom-call.8 = f32[1,128,128]{1,2,0:T(8,128)S(1)} custom-call(f32[1,128,128]{2,1,0:T(8,128)S(1)} %fusion.49), custom_call_target="InvertDiagBlocksLowerTriangular" | custom-call | tf_op jit(solution)/shard_map/triangular_solve/custom-call.0 | solution.py:28
  709.7 0.3 convolution_bitcast_fusion.3
  709.9 1.1 fusion.86
  711.1 0.3 fusion.93
  711.4 0.1 copy.12
  711.5 11.7 %cholesky.85 = f32[128,128]{1,0:T(8,128)S(1)} custom-call(f32[128,128]{1,0:T(8,128)S(1)} %fusion.58), custom_call_target="Cholesky" | custom-call | tf_op jit(solution)/shard_map/jit(cholesky)/cholesky | solution.py:27
  723.2 0.6 compare_reduce_fusion.2
  723.9 0.7 fusion.50
  724.6 10.0 %custom-call.9 = f32[1,128,128]{1,2,0:T(8,128)S(1)} custom-call(f32[1,128,128]{2,1,0:T(8,128)S(1)} %fusion.50), custom_call_target="InvertDiagBlocksLowerTriangular" | custom-call | tf_op jit(solution)/shard_map/triangular_solve/custom-call.0 | solution.py:28
  734.6 0.3 convolution_bitcast_fusion.2
  734.8 1.1 fusion.84
  736.0 0.3 fusion.94
  736.3 0.1 copy.13
  736.4 11.7 %cholesky.96 = f32[128,128]{1,0:T(8,128)S(1)} custom-call(f32[128,128]{1,0:T(8,128)S(1)} %fusion.56), custom_call_target="Cholesky" | custom-call | tf_op jit(solution)/shard_map/jit(cholesky)/cholesky | solution.py:27
  748.1 0.6 compare_reduce_fusion.1
  748.8 0.7 fusion.51
  749.5 9.8 %custom-call.10 = f32[1,128,128]{1,2,0:T(8,128)S(1)} custom-call(f32[1,128,128]{2,1,0:T(8,128)S(1)} %fusion.51), custom_call_target="InvertDiagBlocksLowerTriangular" | custom-call | tf_op jit(solution)/shard_map/triangular_solve/custom-call.0 | solution.py:28
  759.3 0.3 convolution_bitcast_fusion.1
  759.6 1.1 fusion.82
  760.7 0.3 fusion.95
  761.0 0.1 copy.14
  761.1 11.7 %cholesky.107 = f32[128,128]{1,0:T(8,128)S(1)} custom-call(f32[128,128]{1,0:T(8,128)S(1)} %fusion.54), custom_call_target="Cholesky" | custom-call | tf_op jit(solution)/shard_map/jit(cholesky)/cholesky | solution.py:27
  772.9 0.6 compare_reduce_fusion
  773.5 0.7 fusion.52
  774.2 10.0 %custom-call.11 = f32[1,128,128]{1,2,0:T(8,128)S(1)} custom-call(f32[1,128,128]{2,1,0:T(8,128)S(1)} %fusion.52), custom_call_target="InvertDiagBlocksLowerTriangular" | custom-call | tf_op jit(solution)/shard_map/triangular_solve/custom-call.0 | solution.py:28
  784.2 0.2 convolution_bitcast_fusion
  784.4 0.8 fusion.96
  785.2 0.0 copy-done.1
  785.2 0.3 fusion.23
  785.6 1.1 fusion.24
  786.7 0.5 sqrt.3
  787.2 0.8 copy.15
  (12 shorter events, 0.2 us)
Async XLA Ops:
  7.2 678.1 %copy-start = (f32[128,128]{1,0:T(8,128)S(1)}, f32[128,128]{1,0:T(8,128)}, u32[]{:S(2)}) copy-start(f32[128,128]{1,0:T(8,128)} %param.15) | copy-start | bytes 196612
  13.3 19.2 %copy-start.2 = (s32[64,512]{1,0:T(8,128)S(1)}, s32[64,512]{1,0:T(8,128)}, u32[]{:S(2)}) copy-start(s32[64,512]{1,0:T(8,128)} %param.12) | copy-start | bytes 393220
  13.4 19.2 %copy-start.3 = (f32[64,512]{1,0:T(8,128)S(1)}, f32[64,512]{1,0:T(8,128)}, u32[]{:S(2)}) copy-start(f32[64,512]{1,0:T(8,128)} %param.11) | copy-start | bytes 393220
  13.4 388.9 %all-to-all-start = ((bf16[64,512,128]{2,1,0:T(8,128)(2,1)}), bf16[64,512,128]{2,1,0:T(8,128)(2,1)}, u32[]{:S(2)}, u32[]{:S(2)}) async-start(bf16[64,512,128]{2,1,0:T(8,128)(2,1)} %stack.2), calls=%async_computation | async-start | bytes 16777216 | tf_op jit(solution)/shard_map/all_to_all | solution.py:65
  32.5 652.8 %all-reduce.2.cloned.1.call-start = ((), (), s32[]{:S(2)}) async-start(), calls=%async_computation.1 | async-start | bytes 131072 | tf_op jit(solution)/shard_map/psum | solution.py:72
  32.6 10.6 %copy-start.4 = (s32[64]{0:T(128)S(1)}, s32[64]{0:T(128)}, u32[]{:S(2)}) copy-start(s32[64]{0:T(128)} %param.13) | copy-start | bytes 772
  37.6 10.5 %collective-permute-start = (f32[64,3,512]{2,1,0:T(4,128)S(1)}, f32[64,3,512]{2,1,0:T(4,128)S(1)}, u32[]{:S(2)}, u32[]{:S(2)}) collective-permute-start(f32[64,3,512]{2,1,0:T(4,128)S(1)} %get-tuple-element.8), channel_id=1, source_target_pairs={{0,1},{1,2},{2,3},{3,4},{4,5},{5,6},{6,7},{8,9},{9,10},{10,11},{11... | collective-permute-start | bytes 1179656 | tf_op jit(solution)/shard_map/ppermute | solution.py:19
  39.5 10.3 %collective-permute-start.1 = (f32[64,3,512]{2,1,0:T(4,128)S(1)}, f32[64,3,512]{2,1,0:T(4,128)S(1)}, u32[]{:S(2)}, u32[]{:S(2)}) collective-permute-start(f32[64,3,512]{2,1,0:T(4,128)S(1)} %get-tuple-element.9), channel_id=1, source_target_pairs={{1,0},{2,1},{3,2},{4,3},{5,4},{6,5},{7,6},{9,8},{10,9},{11,10},{12... | collective-permute-start | bytes 1179656 | tf_op jit(solution)/shard_map/ppermute | solution.py:20
  59.6 374.2 %copy-start.5 = (f32[128]{0:T(128)S(1)}, f32[128]{0:T(128)}, u32[]{:S(2)}) copy-start(f32[128]{0:T(128)} %param.14) | copy-start | bytes 1540
  59.6 725.6 %copy-start.1 = (bf16[512,128]{1,0:T(8,128)(2,1)S(1)}, bf16[512,128]{1,0:T(8,128)(2,1)}, u32[]{:S(2)}) copy-start(bf16[512,128]{1,0:T(8,128)(2,1)} %param.16) | copy-start | bytes 393220
Sparse Core Ops, SparseCore 0:
  433.9 251.3 all-reduce.1
